TPU v7x, 32 devices: a whole 2x2x4 slice. The times are simulated.
32 devices in a mesh: ctx: 8 (over z, x), exp: 4 (over y, core).
Axes of the slice: x: 2, y: 2, z: 4, core: 2. Of those that a mesh axis runs over, the one named last changes fastest.
Arguments:
- tokens: bfloat16 [2, 1024, 4096], P(None, 'ctx'), may hold values from -1.5 to 1.5
- router: bfloat16 [4096, 2048], P('ctx', 'exp'), may hold values from -8 to 8
- slot_out: bfloat16 [2, 2048, 4096], P(None, 'exp', 'ctx'), may hold values from -6 to 6
- out_grad: bfloat16 [2, 1024, 4096], P(None, 'ctx'), may hold values from -3 to 3
- slot_in_grad: bfloat16 [2, 2048, 4096], P(None, 'exp', 'ctx'), may hold values from -60 to 60
- lengths: int32 [2], replicated, may hold values from 256 to 1024, as said below
Outputs:
- grad_tokens: bfloat16 [2, 1024, 4096], P(None, 'ctx', 'exp')
- grad_router: float32 [4096, 2048], P('ctx', 'exp')
Inputs may be any that keep to these rules, and one draw needn't show every extreme that they name: `lengths`: at least one sequence is valid at all 1024 positions.
All inputs are finite; a program needn't handle non-finite values.
Results may differ from a plain program's by a relative error of at most 0.017.
Values may be sent and summed in bfloat16 or wider, within the bound.
No kernel may reach another device: no remote copies, remote signals or barrier semaphores. Data moves between devices by JAX's collectives and lax.ppermute only.
A program may use at most 64 MiB of HBM per device.

v0:
```python
import jax
import jax.numpy as jnp
from jax import lax
from jax.sharding import PartitionSpec as P

masked_logit = -1e30


def local(tokens, router, slot_out, out_grad, slot_in_grad, lengths):
    seq_count, tok_rows, model_width = tokens.shape
    local_slots = router.shape[1]
    start_row = lax.axis_index("ctx") * tok_rows
    positions = start_row + jnp.arange(tok_rows, dtype=jnp.int32)
    valid_mask = positions[None, :] < lengths[:, None]
    router_full = lax.all_gather(router, "ctx", axis=0, tiled=True)
    flat_tokens = tokens.reshape(seq_count * tok_rows, model_width)
    logits = jnp.dot(flat_tokens, router_full, preferred_element_type=jnp.float32).reshape(
        seq_count, tok_rows, local_slots
    )
    grad_in = jnp.where(valid_mask[:, :, None], out_grad, jnp.zeros((), out_grad.dtype))
    comb_grad = jnp.einsum(
        "bnd,bsd->bns",
        grad_in,
        lax.all_gather(slot_out, "ctx", axis=2, tiled=True),
        preferred_element_type=jnp.float32,
    )
    grads_full = lax.all_gather(slot_in_grad, "ctx", axis=2, tiled=True)
    disp_grad = jnp.einsum("bnd,bsd->bns", tokens, grads_full, preferred_element_type=jnp.float32)
    local_peak = jnp.max(logits, axis=2)
    shifted = jnp.exp(logits - local_peak[:, :, None])
    local_total = jnp.sum(shifted, axis=2)
    local_weighted = jnp.sum(shifted * comb_grad, axis=2)
    masked = jnp.where(valid_mask[:, :, None], logits, masked_logit)
    slot_peak = jnp.max(masked, axis=1)
    slot_shift = jnp.where(valid_mask[:, :, None], jnp.exp(masked - slot_peak[:, None, :]), 0.0)
    slot_total = jnp.sum(slot_shift, axis=1)
    slot_weighted = jnp.sum(slot_shift * disp_grad, axis=1)
    comb_peak = lax.pmax(local_peak, "exp")
    disp_peak = lax.pmax(slot_peak, "ctx")
    comb_rescale = jnp.exp(local_peak - comb_peak)
    comb_total, comb_weighted = lax.psum(
        (local_total * comb_rescale, local_weighted * comb_rescale), "exp"
    )
    disp_rescale = jnp.exp(slot_peak - disp_peak)
    disp_total, disp_weighted = lax.psum(
        (slot_total * disp_rescale, slot_weighted * disp_rescale), "ctx"
    )
    combine = jnp.exp(logits - comb_peak[:, :, None]) / comb_total[:, :, None]
    comb_mean = comb_weighted / comb_total
    dispatch = jnp.where(
        valid_mask[:, :, None],
        jnp.exp(masked - disp_peak[:, None, :]) / disp_total[:, None, :],
        0.0,
    )
    disp_mean = disp_weighted / disp_total
    grad_logits = combine * (comb_grad - comb_mean[:, :, None]) + dispatch * (
        disp_grad - disp_mean[:, None, :]
    )
    logit_low = grad_logits.astype(jnp.bfloat16)
    dispatch_low = dispatch.astype(jnp.bfloat16)

    def router_term(amount):
        running = jnp.zeros((amount, local_slots), jnp.float32)
        for seq_index in range(seq_count):

            def compute(seq_index=seq_index):
                return jnp.einsum(
                    "nd,ns->ds",
                    tokens[seq_index],
                    logit_low[seq_index],
                    preferred_element_type=jnp.float32,
                )

            running = running + compute()
        return running

    grad_router = lax.psum_scatter(
        router_term(router.shape[0] * lax.axis_size("ctx")).astype(jnp.bfloat16),
        "ctx",
        scatter_dimension=0,
        tiled=True,
    ).astype(jnp.float32)
    blocks = []
    for seq_index in range(seq_count):

        def compute(seq_index=seq_index):
            first = jnp.dot(
                dispatch_low[seq_index], grads_full[seq_index], preferred_element_type=jnp.float32
            )
            return first + jnp.einsum(
                "ns,ds->nd", logit_low[seq_index], router_full, preferred_element_type=jnp.float32
            )

        blocks.append(compute())
    partial_grad = jnp.stack(blocks)
    grad_tokens = lax.psum_scatter(
        partial_grad.astype(jnp.bfloat16), "exp", scatter_dimension=2, tiled=True
    )
    return (grad_tokens, grad_router)


def solution(mesh):
    return jax.shard_map(
        local,
        mesh=mesh,
        in_specs=(
            P(None, "ctx", None),
            P("ctx", "exp"),
            P(None, "exp", "ctx"),
            P(None, "ctx", None),
            P(None, "exp", "ctx"),
            P(),
        ),
        out_specs=(P(None, "ctx", "exp"), P("ctx", "exp")),
        check_vma=False,
    )
```

profile of v0, /device:TPU:0, one launch (start us, length us, event | category | flops | bytes accessed | tf_op | source)
XLA Modules:
  0.0 502.1 jit_solution(17626797504241054919)
XLA Ops:
  7.2 0.7 all-gather.4.cloned.1.call-update
  7.9 0.7 all-gather.6.cloned.1.call-update
  9.4 0.7 broadcast_compare_fusion
  10.2 75.5 %all-gather.4.cloned.1.call-done = bf16[4096,512]{1,0:T(8,128)(2,1)} async-done(((bf16[512,512]{1,0:T(8,128)(2,1)}), bf16[4096,512]{1,0:T(8,128)(2,1)}) %all-gather.4.cloned.1.call-update) | async-done | bytes 4194320 | tf_op jit(solution)/shard_map/all_gather | solution.py:15
  85.6 4.2 fusion.26
  89.8 5.7 %pmax.15 = f32[2,128]{1,0:T(2,128)S(1)} all-reduce(f32[2,128]{1,0:T(2,128)S(1)} %get-tuple-element.10), channel_id=1, replica_groups=mesh['ctx'=8,'exp'=4] {'exp'}, use_global_device_ids=true, to_apply=%region_5.6 | all-reduce | flops 256 | bytes 2048 | tf_op jit(solution)/shard_map/pmax | solution.py:38
  95.5 20.5 %pmax.14 = f32[2,512]{1,0:T(2,128)S(1)} all-reduce(f32[2,512]{1,0:T(2,128)S(1)} %get-tuple-element.11), channel_id=1, replica_groups=mesh['ctx'=8,'exp'=4] {'ctx'}, use_global_device_ids=true, to_apply=%region_1.2 | all-reduce | flops 1024 | bytes 8192 | tf_op jit(solution)/shard_map/pmax | solution.py:39
  116.0 95.7 %all-gather.6.cloned.1.call-done = bf16[2,512,4096]{2,1,0:T(8,128)(2,1)} async-done(((bf16[2,512,512]{2,1,0:T(8,128)(2,1)}), bf16[2,512,4096]{2,1,0:T(8,128)(2,1)}) %all-gather.6.cloned.1.call-update) | async-done | bytes 8388624 | tf_op jit(solution)/shard_map/all_gather | solution.py:27
  211.7 6.3 %fusion.27 = f32[2,128,512]{2,1,0:T(8,128)S(1)} fusion(bf16[2,128,4096]{2,1,0:T(8,128)(2,1)S(1)} %copy-done.1, bf16[2,512,4096]{2,1,0:T(8,128)(2,1)} %all-gather.6.cloned.1.call-done), kind=kOutput, calls=%fused_computation.48 | convolution fusion | flops 1073741824 | bytes 11010048 | tf_op jit(solution)/shard_map/bnd,bsd->bns/dot_general | solution.py:28
  218.0 118.9 %all-gather.8.cloned.1.call-done = bf16[2,512,4096]{2,1,0:T(8,128)(2,1)} async-done(((bf16[2,512,512]{2,1,0:T(8,128)(2,1)}), bf16[2,512,4096]{2,1,0:T(8,128)(2,1)}) %all-gather.8.cloned.1.call-update) | async-done | bytes 8388624 | tf_op jit(solution)/shard_map/all_gather | solution.py:24
  336.9 7.8 %fusion.18 = (f32[2,128]{1,0:T(2,128)S(1)}, f32[2,128]{1,0:T(2,128)S(1)}, f32[2,512]{1,0:T(2,128)S(1)}, f32[2,512]{1,0:T(2,128)S(1)}, f32[2,128,512]{2,1,0:T(8,128)}) fusion(f32[2,128,512]{2,1,0:T(8,128)S(1)} %get-tuple-element.22, f32[2,128]{1,0:T(2,128)S(1)} %get-tuple-element.10, f32[2,512]{1,0:T(2,128)S(1)} %get-tuple-element.11, ...), kind=kOutput, calls=%fused_computation.30 | convolution fusion | flops 1076098560 | bytes 12074240 | tf_op jit(solution)/shard_map/bnd,bsd->bns/dot_general | solution.py:21
  344.7 5.9 %all-reduce.1 = (f32[2,128]{1,0:T(2,128)S(1)}, f32[2,128]{1,0:T(2,128)S(1)}) all-reduce(f32[2,128]{1,0:T(2,128)S(1)} %get-tuple-element.21, f32[2,128]{1,0:T(2,128)S(1)} %get-tuple-element.20), channel_id=1, replica_groups=mesh['ctx'=8,'exp'=4] {'exp'}, use_global_device_ids=true, to_apply=%region_9.10 | all-reduce | flops 512 | bytes 4096 | tf_op jit(solution)/shard_map/psum | solution.py:41
  350.6 19.8 %all-reduce = (f32[2,512]{1,0:T(2,128)S(1)}, f32[2,512]{1,0:T(2,128)S(1)}) all-reduce(f32[2,512]{1,0:T(2,128)S(1)} %get-tuple-element.19, f32[2,512]{1,0:T(2,128)S(1)} %get-tuple-element.18), channel_id=1, replica_groups=mesh['ctx'=8,'exp'=4] {'ctx'}, use_global_device_ids=true, to_apply=%region_11.12 | all-reduce | flops 2048 | bytes 16384 | tf_op jit(solution)/shard_map/psum | solution.py:45
  370.4 1.6 add_convert_fusion.1
  372.0 1.3 fusion.13
  373.3 3.3 fusion
  376.6 2.9 fusion.5
  379.5 3.3 fusion.6
  383.3 1.5 fusion.4
  384.8 1.5 fusion.3
  386.3 1.5 pad_maximum_fusion
  387.8 74.0 %reduce-scatter.5.cloned.1.call-done = bf16[512,512]{0,1:T(8,128)(2,1)} async-done(((bf16[4096,512]{0,1:T(8,128)(2,1)}), bf16[512,512]{0,1:T(8,128)(2,1)}) %reduce-scatter.5.cloned.1.call-update) | async-done | bytes 524304 | tf_op jit(solution)/shard_map/reduce_scatter | solution.py:77
  461.8 2.2 copy.8
  464.0 31.6 %reduce-scatter.3.cloned.1.call-done = bf16[2,128,1024]{2,1,0:T(8,128)(2,1)} async-done(((bf16[2,128,4096]{2,1,0:T(8,128)(2,1)}), bf16[2,128,1024]{2,1,0:T(8,128)(2,1)}) %reduce-scatter.3.cloned.1.call-update) | async-done | bytes 524304 | tf_op jit(solution)/shard_map/reduce_scatter | solution.py:96
  (19 shorter events, 1.4 us)
Async XLA Ops:
  7.2 78.5 %all-gather.4.cloned.1.call-start = ((), (), s32[]{:S(2)}) async-start(), calls=%async_computation.2 | async-start | bytes 4718592 | tf_op jit(solution)/shard_map/all_gather | solution.py:15
  7.9 203.8 %all-gather.6.cloned.1.call-start = ((), (), s32[]{:S(2)}) async-start(), calls=%async_computation.3 | async-start | bytes 9437184 | tf_op jit(solution)/shard_map/all_gather | solution.py:27
  8.6 328.3 %all-gather.8.cloned.1.call-start = ((), (), s32[]{:S(2)}) async-start(), calls=%async_computation.4 | async-start | bytes 9437184 | tf_op jit(solution)/shard_map/all_gather | solution.py:24
  9.4 452.4 %reduce-scatter.5.cloned.1.call-start = ((), (), s32[]{:S(2)}) async-start(), calls=%async_computation.6 | async-start | bytes 4718592 | tf_op jit(solution)/shard_map/reduce_scatter | solution.py:77
  10.2 201.5 %copy-start.1 = (bf16[2,128,4096]{2,1,0:T(8,128)(2,1)S(1)}, bf16[2,128,4096]{2,1,0:T(8,128)(2,1)}, u32[]{:S(2)}) copy-start(bf16[2,128,4096]{2,1,0:T(8,128)(2,1)} %param.6) | copy-start | bytes 6291460
  89.8 247.1 %copy-start.2 = (f32[2,128,512]{2,1,0:T(8,128)}, f32[2,128,512]{2,1,0:T(8,128)S(1)}, u32[]{:S(2)}) copy-start(f32[2,128,512]{2,1,0:T(8,128)S(1)} %get-tuple-element.22) | copy-start | bytes 1572868
  376.6 119.0 %reduce-scatter.3.cloned.1.call-start = ((), (), s32[]{:S(2)}) async-start(), calls=%async_computation.5 | async-start | bytes 2621440 | tf_op jit(solution)/shard_map/reduce_scatter | solution.py:96
  379.5 3.7 copy-start
Sparse Core Ops, SparseCore 0:
  10.1 75.4 all-gather.3
  87.7 123.9 all-gather.5
  213.8 123.1 all-gather.7
  376.7 85.0 reduce-scatter.4
  464.8 30.8 reduce-scatter.2
where the time goes:
time: 502 us
  waiting for transfers between devices  398 us (79%)
  blocking collectives  51.9 us (10%)
  matrix products  31.9 us (6%)
  between operations  13.9 us (3%)
    all_gather x1, waiting for transfers between devices, local(): lax.all_gather(slot_out, 'ctx', axis=2, tiled=True)  119 us
    all_gather x1, waiting for transfers between devices, local(): grads_full = lax.all_gather(slot_in_grad, 'ctx', axis=2, tiled=True)  95.7 us
    all_gather x1, waiting for transfers between devices, local(): router_full = lax.all_gather(router, 'ctx', axis=0, tiled=True)  75.5 us
    reduce_scatter x1, waiting for transfers between devices, local(): lax.psum_scatter(router_term(router.shape[0] * lax.axis_size('ctx')).asty...  74 us
    reduce_scatter x1, waiting for transfers between devices, local(): lax.psum_scatter(partial_grad.astype(jnp.bfloat16), 'exp', scatter_dimens...  31.6 us
    pmax x1, blocking collectives, local(): disp_peak = lax.pmax(slot_peak, 'ctx')  20.5 us
    psum x1, blocking collectives, local(): lax.psum((slot_total * disp_rescale, slot_weighted * disp_rescale), 'ctx')  19.8 us
  transfers between devices with their start and end apart: 5, of which 5 were waited for; matrix products, arithmetic and copies ran while one was open for 5% of the time, Pallas kernels for 0%

commit v1 on v0

--- a/solution.py
+++ b/solution.py
@@ -12,7 +12,13 @@
     start_row = lax.axis_index("ctx") * tok_rows
     positions = start_row + jnp.arange(tok_rows, dtype=jnp.int32)
     valid_mask = positions[None, :] < lengths[:, None]
-    router_full = lax.all_gather(router, "ctx", axis=0, tiled=True)
+    count = lax.axis_size("ctx")
+    held, parts = (router, [router])
+    for _ in range(count - 1):
+        held = lax.ppermute(held, "ctx", [(i, (i + 1) % count) for i in range(count)])
+        parts.insert(0, held)
+    row_of_blocks = jnp.concatenate(parts, axis=0)
+    router_full = jnp.roll(row_of_blocks, (lax.axis_index("ctx") + 1) * router.shape[0], axis=0)
     flat_tokens = tokens.reshape(seq_count * tok_rows, model_width)
     logits = jnp.dot(flat_tokens, router_full, preferred_element_type=jnp.float32).reshape(
         seq_count, tok_rows, local_slots

time: 502 us -> 471 us (0.938)
  waiting for transfers between devices: 398 us -> 320 us
  starting transfers between devices: 0.19 us -> 19.3 us
  blocking collectives: 51.9 us -> 66.7 us
  local copies, waits for them, and re-layouts: 2.69 us -> 15.2 us
    ppermute x0 -> x7, waiting for transfers between devices: none -> 157 us  [local(): lax.ppermute(held, 'ctx', [(i, (i + 1) % count) for i in range(count)])]
    all_gather x1, waiting for transfers between devices: 95.7 us -> 0.02 us  [local(): grads_full = lax.all_gather(slot_in_grad, 'ctx', axis=2, tiled=True)]
    all_gather x1 -> x0, waiting for transfers between devices: 75.5 us -> none  [local(): router_full = lax.all_gather(router, 'ctx', axis=0, tiled=True)]
    all_gather x1, waiting for transfers between devices: 119 us -> 56.3 us  [local(): lax.all_gather(slot_out, 'ctx', axis=2, tiled=True)]
    ppermute x0 -> x7, starting transfers between devices: none -> 19 us  [local(): lax.ppermute(held, 'ctx', [(i, (i + 1) % count) for i in range(count)])]
    pmax x1, blocking collectives: 20.5 us -> 34.9 us  [local(): disp_peak = lax.pmax(slot_peak, 'ctx')]
    unnamed x7 -> x46, local copies, waits for them, and re-layouts: 2.69 us -> 15.2 us
  transfers between devices with their start and end apart: 5 -> 11, of which waited for: 5 -> 10; matrix products, arithmetic and copies ran while one was open for 5% -> 7% of each run, Pallas kernels for 0% -> 0%
where the time goes in v1:
time: 471 us
  waiting for transfers between devices  320 us (68%)
  blocking collectives  66.7 us (14%)
  matrix products  30.5 us (6%)
  starting transfers between devices  19.3 us (4%)
  local copies, waits for them, and re-layouts  15.2 us (3%)
  between operations  14.1 us (3%)
  other arithmetic  4.98 us (1%)
    ppermute x7, waiting for transfers between devices, local(): lax.ppermute(held, 'ctx', [(i, (i + 1) % count) for i in range(count)])  157 us
    reduce_scatter x1, waiting for transfers between devices, local(): lax.psum_scatter(router_term(router.shape[0] * lax.axis_size('ctx')).asty...  73.7 us
    all_gather x1, waiting for transfers between devices, local(): lax.all_gather(slot_out, 'ctx', axis=2, tiled=True)  56.3 us
    pmax x1, blocking collectives, local(): disp_peak = lax.pmax(slot_peak, 'ctx')  34.9 us
    reduce_scatter x1, waiting for transfers between devices, local(): lax.psum_scatter(partial_grad.astype(jnp.bfloat16), 'exp', scatter_dimens...  31.6 us
    psum x1, blocking collectives, local(): lax.psum((slot_total * disp_rescale, slot_weighted * disp_rescale), 'ctx')  20.1 us
    ppermute x7, starting transfers between devices, local(): lax.ppermute(held, 'ctx', [(i, (i + 1) % count) for i in range(count)])  19 us
    unnamed x46, local copies, waits for them, and re-layouts  15.2 us
  transfers between devices with their start and end apart: 11, of which 10 were waited for; matrix products, arithmetic and copies ran while one was open for 7% of the time, Pallas kernels for 0%

profile of v1, /device:TPU:0, one launch (start us, length us, event | category | flops | bytes accessed | tf_op | source)
XLA Modules:
  0.0 470.5 jit_solution(7663898905694833167)
XLA Ops:
  8.7 3.0 collective-permute-start
  11.7 15.3 %collective-permute-done = bf16[512,512]{1,0:T(8,128)(2,1)S(1)} collective-permute-done((bf16[512,512]{1,0:T(8,128)(2,1)}, bf16[512,512]{1,0:T(8,128)(2,1)S(1)}, u32[]{:S(2)}, u32[]{:S(2)}) %collective-permute-start) | collective-permute-done | bytes 524320 | tf_op jit(solution)/shard_map/ppermute | solution.py:18
  28.2 22.6 %collective-permute-done.1 = bf16[512,512]{1,0:T(8,128)(2,1)S(1)} collective-permute-done((bf16[512,512]{1,0:T(8,128)(2,1)S(1)}, bf16[512,512]{1,0:T(8,128)(2,1)S(1)}, u32[]{:S(2)}, u32[]{:S(2)}) %collective-permute-start.1) | collective-permute-done | bytes 524320 | tf_op jit(solution)/shard_map/ppermute | solution.py:18
  50.8 27.9 %collective-permute-done.2 = bf16[512,512]{1,0:T(8,128)(2,1)S(1)} collective-permute-done((bf16[512,512]{1,0:T(8,128)(2,1)S(1)}, bf16[512,512]{1,0:T(8,128)(2,1)S(1)}, u32[]{:S(2)}, u32[]{:S(2)}) %collective-permute-start.2) | collective-permute-done | bytes 524320 | tf_op jit(solution)/shard_map/ppermute | solution.py:18
  78.7 18.3 %collective-permute-done.3 = bf16[512,512]{1,0:T(8,128)(2,1)S(1)} collective-permute-done((bf16[512,512]{1,0:T(8,128)(2,1)S(1)}, bf16[512,512]{1,0:T(8,128)(2,1)S(1)}, u32[]{:S(2)}, u32[]{:S(2)}) %collective-permute-start.3) | collective-permute-done | bytes 524320 | tf_op jit(solution)/shard_map/ppermute | solution.py:18
  97.0 27.3 %collective-permute-done.4 = bf16[512,512]{1,0:T(8,128)(2,1)S(1)} collective-permute-done((bf16[512,512]{1,0:T(8,128)(2,1)S(1)}, bf16[512,512]{1,0:T(8,128)(2,1)S(1)}, u32[]{:S(2)}, u32[]{:S(2)}) %collective-permute-start.4) | collective-permute-done | bytes 524320 | tf_op jit(solution)/shard_map/ppermute | solution.py:18
  124.9 27.0 %collective-permute-done.5 = bf16[512,512]{1,0:T(8,128)(2,1)} collective-permute-done((bf16[512,512]{1,0:T(8,128)(2,1)S(1)}, bf16[512,512]{1,0:T(8,128)(2,1)}, u32[]{:S(2)}, u32[]{:S(2)}) %collective-permute-start.5) | collective-permute-done | bytes 524320 | tf_op jit(solution)/shard_map/ppermute | solution.py:18
  151.9 14.3 %collective-permute-start.6 = (bf16[512,512]{1,0:T(8,128)(2,1)}, bf16[512,512]{1,0:T(8,128)(2,1)}, u32[]{:S(2)}, u32[]{:S(2)}) collective-permute-start(bf16[512,512]{1,0:T(8,128)(2,1)} %collective-permute-done.5), channel_id=1, source_target_pairs={{0,4},{4,8},{8,12},{12,16},{16,20},{20,24},{24,28},{28,0},{1,5},{5... | collective-permute-start | bytes 1572872 | tf_op jit(solution)/shard_map/ppermute | solution.py:18
  166.9 18.3 %collective-permute-done.6 = bf16[512,512]{1,0:T(8,128)(2,1)} collective-permute-done((bf16[512,512]{1,0:T(8,128)(2,1)}, bf16[512,512]{1,0:T(8,128)(2,1)}, u32[]{:S(2)}, u32[]{:S(2)}) %collective-permute-start.6) | collective-permute-done | bytes 524320 | tf_op jit(solution)/shard_map/ppermute | solution.py:18
  194.3 3.2 copy-done
  198.9 5.7 %pmax.15 = f32[2,128]{1,0:T(2,128)S(1)} all-reduce(f32[2,128]{1,0:T(2,128)S(1)} %bitcast.59), channel_id=1, replica_groups=mesh['ctx'=8,'exp'=4] {'exp'}, use_global_device_ids=true, to_apply=%region_5.6 | all-reduce | flops 256 | bytes 2048 | tf_op jit(solution)/shard_map/pmax | solution.py:44
  204.5 34.9 %pmax.14 = f32[2,512]{1,0:T(2,128)S(1)} all-reduce(f32[2,512]{1,0:T(2,128)S(1)} %get-tuple-element.16), channel_id=1, replica_groups=mesh['ctx'=8,'exp'=4] {'ctx'}, use_global_device_ids=true, to_apply=%region_1.2 | all-reduce | flops 1024 | bytes 8192 | tf_op jit(solution)/shard_map/pmax | solution.py:45
  239.7 6.3 %multiply_reduce_fusion = (f32[2,512]{1,0:T(2,128)S(1)}, f32[2,512]{1,0:T(2,128)S(1)}, f32[2,128,512]{2,1,0:T(8,128)S(1)}) fusion(f32[2,512]{1,0:T(2,128)S(1)} %get-tuple-element.16, pred[2,128]{1,0:T(4,128)(4,1)S(1)} %broadcast_compare_fusion, f32[512,256]{0,1:T(8,128)S(1)} %get-tuple-element.17, bf16[2,128,4096]{2,1,0:T(8,128)(2,1)S(1)} %copy-done.1, ...), kind=kOutput, calls=%fused_computation.30 | convolution fusion | flops 1074526208 | bytes 11546880 | tf_op jit(solution)/shard_map/bnd,bsd->bns/dot_general | solution.py:34
  246.0 20.1 %all-reduce = (f32[2,512]{1,0:T(2,128)S(1)}, f32[2,512]{1,0:T(2,128)S(1)}) all-reduce(f32[2,512]{1,0:T(2,128)S(1)} %get-tuple-element.13, f32[2,512]{1,0:T(2,128)S(1)} %get-tuple-element.12), channel_id=1, replica_groups=mesh['ctx'=8,'exp'=4] {'ctx'}, use_global_device_ids=true, to_apply=%region_11.12 | all-reduce | flops 2048 | bytes 16384 | tf_op jit(solution)/shard_map/psum | solution.py:51
  266.1 56.3 %all-gather.5.cloned.1.call-done = bf16[2,512,4096]{2,1,0:T(8,128)(2,1)} async-done(((bf16[2,512,512]{2,1,0:T(8,128)(2,1)}), bf16[2,512,4096]{2,1,0:T(8,128)(2,1)}) %all-gather.5.cloned.1.call-update) | async-done | bytes 8388624 | tf_op jit(solution)/shard_map/all_gather | solution.py:30
  322.4 6.9 %fusion.11 = f32[2,128,512]{2,1,0:T(8,128)S(1)} fusion(bf16[2,512,4096]{2,1,0:T(8,128)(2,1)} %all-gather.5.cloned.1.call-done, bf16[2,128,4096]{2,1,0:T(8,128)(2,1)} %param.9, pred[2,128]{1,0:T(4,128)(4,1)S(1)} %broadcast_compare_fusion), kind=kOutput, calls=%fused_computation.17 | convolution fusion | flops 1074790400 | bytes 11010304 | tf_op jit(solution)/shard_map/bnd,bsd->bns/dot_general | solution.py:27
  330.4 6.1 %all-reduce.1 = (f32[2,128]{1,0:T(2,128)S(1)}, f32[2,128]{1,0:T(2,128)S(1)}) all-reduce(f32[2,128]{1,0:T(2,128)S(1)} %get-tuple-element.15, f32[2,128]{1,0:T(2,128)S(1)} %get-tuple-element.14), channel_id=1, replica_groups=mesh['ctx'=8,'exp'=4] {'exp'}, use_global_device_ids=true, to_apply=%region_9.10 | all-reduce | flops 512 | bytes 4096 | tf_op jit(solution)/shard_map/psum | solution.py:47
  339.9 3.3 fusion
  343.4 3.1 fusion.5
  346.5 4.0 fusion.3
  350.5 2.9 fusion.6
  356.5 73.7 %reduce-scatter.5.cloned.1.call-done = bf16[512,512]{0,1:T(8,128)(2,1)} async-done(((bf16[4096,512]{0,1:T(8,128)(2,1)}), bf16[512,512]{0,1:T(8,128)(2,1)}) %reduce-scatter.5.cloned.1.call-update) | async-done | bytes 524304 | tf_op jit(solution)/shard_map/reduce_scatter | solution.py:83
  430.2 2.2 copy.8
  432.4 31.6 %reduce-scatter.3.cloned.1.call-done = bf16[2,128,1024]{2,1,0:T(8,128)(2,1)} async-done(((bf16[2,128,4096]{2,1,0:T(8,128)(2,1)}), bf16[2,128,1024]{2,1,0:T(8,128)(2,1)}) %reduce-scatter.3.cloned.1.call-update) | async-done | bytes 524304 | tf_op jit(solution)/shard_map/reduce_scatter | solution.py:102
  (74 shorter events, 22.2 us)
Async XLA Ops:
  7.2 184.6 %copy-start.3 = (bf16[512,512]{1,0:T(8,128)(2,1)S(1)}, bf16[512,512]{1,0:T(8,128)(2,1)}, u32[]{:S(2)}) copy-start(bf16[512,512]{1,0:T(8,128)(2,1)} %param.7) | copy-start | bytes 1572868
  7.2 232.5 %all-gather.3.cloned.1.call-start = ((), (), s32[]{:S(2)}) async-start(), calls=%async_computation.2 | async-start | bytes 9437184 | tf_op jit(solution)/shard_map/all_gather | solution.py:33
  7.9 314.5 %all-gather.5.cloned.1.call-start = ((), (), s32[]{:S(2)}) async-start(), calls=%async_computation.3 | async-start | bytes 9437184 | tf_op jit(solution)/shard_map/all_gather | solution.py:30
  8.7 421.5 %reduce-scatter.5.cloned.1.call-start = ((), (), s32[]{:S(2)}) async-start(), calls=%async_computation.5 | async-start | bytes 4718592 | tf_op jit(solution)/shard_map/reduce_scatter | solution.py:83
  8.7 18.3 %collective-permute-start = (bf16[512,512]{1,0:T(8,128)(2,1)}, bf16[512,512]{1,0:T(8,128)(2,1)S(1)}, u32[]{:S(2)}, u32[]{:S(2)}) collective-permute-start(bf16[512,512]{1,0:T(8,128)(2,1)} %param.7), channel_id=1, source_target_pairs={{0,4},{4,8},{8,12},{12,16},{16,20},{20,24},{24,28},{28,0},{1,5},{5... | collective-permute-start | bytes 1572872 | tf_op jit(solution)/shard_map/ppermute | solution.py:18
  27.0 23.8 %collective-permute-start.1 = (bf16[512,512]{1,0:T(8,128)(2,1)S(1)}, bf16[512,512]{1,0:T(8,128)(2,1)S(1)}, u32[]{:S(2)}, u32[]{:S(2)}) collective-permute-start(bf16[512,512]{1,0:T(8,128)(2,1)S(1)} %collective-permute-done), channel_id=1, source_target_pairs={{0,4},{4,8},{8,12},{12,16},{16,20},{20,24},{24,28},{28,0},{1,5},{5... | collective-permute-start | bytes 1572872 | tf_op jit(solution)/shard_map/ppermute | solution.py:18
  50.8 115.4 %copy-start.4 = (bf16[512,512]{1,0:T(8,128)(2,1)}, bf16[512,512]{1,0:T(8,128)(2,1)S(1)}, u32[]{:S(2)}) copy-start(bf16[512,512]{1,0:T(8,128)(2,1)S(1)} %collective-permute-done.1) | copy-start | bytes 1572868
  50.8 27.9 %collective-permute-start.2 = (bf16[512,512]{1,0:T(8,128)(2,1)S(1)}, bf16[512,512]{1,0:T(8,128)(2,1)S(1)}, u32[]{:S(2)}, u32[]{:S(2)}) collective-permute-start(bf16[512,512]{1,0:T(8,128)(2,1)S(1)} %collective-permute-done.1), channel_id=1, source_target_pairs={{0,4},{4,8},{8,12},{12,16},{16,20},{20,24},{24,28},{28,0},{1,5},{5... | collective-permute-start | bytes 1572872 | tf_op jit(solution)/shard_map/ppermute | solution.py:18
  78.7 87.4 %copy-start.6 = (bf16[512,512]{1,0:T(8,128)(2,1)}, bf16[512,512]{1,0:T(8,128)(2,1)S(1)}, u32[]{:S(2)}) copy-start(bf16[512,512]{1,0:T(8,128)(2,1)S(1)} %collective-permute-done.2) | copy-start | bytes 1572868
  78.7 18.3 %collective-permute-start.3 = (bf16[512,512]{1,0:T(8,128)(2,1)S(1)}, bf16[512,512]{1,0:T(8,128)(2,1)S(1)}, u32[]{:S(2)}, u32[]{:S(2)}) collective-permute-start(bf16[512,512]{1,0:T(8,128)(2,1)S(1)} %collective-permute-done.2), channel_id=1, source_target_pairs={{0,4},{4,8},{8,12},{12,16},{16,20},{20,24},{24,28},{28,0},{1,5},{5... | collective-permute-start | bytes 1572872 | tf_op jit(solution)/shard_map/ppermute | solution.py:18
  97.0 69.1 %copy-start.8 = (bf16[512,512]{1,0:T(8,128)(2,1)}, bf16[512,512]{1,0:T(8,128)(2,1)S(1)}, u32[]{:S(2)}) copy-start(bf16[512,512]{1,0:T(8,128)(2,1)S(1)} %collective-permute-done.3) | copy-start | bytes 1572868
  97.0 27.3 %collective-permute-start.4 = (bf16[512,512]{1,0:T(8,128)(2,1)S(1)}, bf16[512,512]{1,0:T(8,128)(2,1)S(1)}, u32[]{:S(2)}, u32[]{:S(2)}) collective-permute-start(bf16[512,512]{1,0:T(8,128)(2,1)S(1)} %collective-permute-done.3), channel_id=1, source_target_pairs={{0,4},{4,8},{8,12},{12,16},{16,20},{20,24},{24,28},{28,0},{1,5},{5... | collective-permute-start | bytes 1572872 | tf_op jit(solution)/shard_map/ppermute | solution.py:18
  124.3 41.9 %copy-start.10 = (bf16[512,512]{1,0:T(8,128)(2,1)}, bf16[512,512]{1,0:T(8,128)(2,1)S(1)}, u32[]{:S(2)}) copy-start(bf16[512,512]{1,0:T(8,128)(2,1)S(1)} %collective-permute-done.4) | copy-start | bytes 1572868
  124.3 27.6 %collective-permute-start.5 = (bf16[512,512]{1,0:T(8,128)(2,1)S(1)}, bf16[512,512]{1,0:T(8,128)(2,1)}, u32[]{:S(2)}, u32[]{:S(2)}) collective-permute-start(bf16[512,512]{1,0:T(8,128)(2,1)S(1)} %collective-permute-done.4), channel_id=1, source_target_pairs={{0,4},{4,8},{8,12},{12,16},{16,20},{20,24},{24,28},{28,0},{1,5},{5... | collective-permute-start | bytes 1572872 | tf_op jit(solution)/shard_map/ppermute | solution.py:18
  151.9 33.3 %collective-permute-start.6 = (bf16[512,512]{1,0:T(8,128)(2,1)}, bf16[512,512]{1,0:T(8,128)(2,1)}, u32[]{:S(2)}, u32[]{:S(2)}) collective-permute-start(bf16[512,512]{1,0:T(8,128)(2,1)} %collective-permute-done.5), channel_id=1, source_target_pairs={{0,4},{4,8},{8,12},{12,16},{16,20},{20,24},{24,28},{28,0},{1,5},{5... | collective-permute-start | bytes 1572872 | tf_op jit(solution)/shard_map/ppermute | solution.py:18
  166.9 27.0 %copy-start.11 = (bf16[512,512]{1,0:T(8,128)(2,1)S(1)}, bf16[512,512]{1,0:T(8,128)(2,1)}, u32[]{:S(2)}) copy-start(bf16[512,512]{1,0:T(8,128)(2,1)} %copy-done.10) | copy-start | bytes 1572868
  166.9 27.1 %copy-start.9 = (bf16[512,512]{1,0:T(8,128)(2,1)S(1)}, bf16[512,512]{1,0:T(8,128)(2,1)}, u32[]{:S(2)}) copy-start(bf16[512,512]{1,0:T(8,128)(2,1)} %copy-done.8) | copy-start | bytes 1572868
  166.9 27.1 %copy-start.7 = (bf16[512,512]{1,0:T(8,128)(2,1)S(1)}, bf16[512,512]{1,0:T(8,128)(2,1)}, u32[]{:S(2)}) copy-start(bf16[512,512]{1,0:T(8,128)(2,1)} %copy-done.6) | copy-start | bytes 1572868
  166.9 27.2 %copy-start.5 = (bf16[512,512]{1,0:T(8,128)(2,1)S(1)}, bf16[512,512]{1,0:T(8,128)(2,1)}, u32[]{:S(2)}) copy-start(bf16[512,512]{1,0:T(8,128)(2,1)} %copy-done.4) | copy-start | bytes 1572868
  166.9 30.6 %copy-start.1 = (bf16[2,128,4096]{2,1,0:T(8,128)(2,1)S(1)}, bf16[2,128,4096]{2,1,0:T(8,128)(2,1)}, u32[]{:S(2)}) copy-start(bf16[2,128,4096]{2,1,0:T(8,128)(2,1)} %param.6) | copy-start | bytes 6291460
  339.9 3.5 copy-start.12
  343.2 120.8 %reduce-scatter.3.cloned.1.call-start = ((), (), s32[]{:S(2)}) async-start(), calls=%async_computation.4 | async-start | bytes 2621440 | tf_op jit(solution)/shard_map/reduce_scatter | solution.py:102
  343.4 10.0 %slice-start = ((s8[8388608]{0:T(1024)(128)(4,1)}), s8[4194304]{0:T(1024)(128)(4,1)S(1)}, s32[]{:S(2)}) async-start(s8[8388608]{0:T(1024)(128)(4,1)} %bitcast.55), calls=%async_computation.6 | async-start | bytes 8388608
  346.5 6.9 %slice-start.1 = ((s8[8388608]{0:T(1024)(128)(4,1)}), s8[4194304]{0:T(1024)(128)(4,1)S(1)}, s32[]{:S(2)}) async-start(s8[8388608]{0:T(1024)(128)(4,1)} %bitcast.55), calls=%async_computation.7 | async-start | bytes 8388608
  (2 other events, 4.0 us)
Sparse Core Ops, SparseCore 0:
  10.0 178.9 all-gather.2
  191.0 131.3 all-gather.4
  343.3 86.8 reduce-scatter.4
  433.1 30.8 reduce-scatter.2
